TPU v7x, 128 devices: a whole 4x4x4 slice. The times are simulated.
128 devices in a mesh: dp: 4 (over x), seq: 8 (over z, core), tensor: 4 (over y).
Axes of the slice: x: 4, y: 4, z: 4, core: 2. Of those that a mesh axis runs over, the one named last changes fastest.
Arguments:
- block_input: bfloat16 [2048, 4, 1024], P('seq', 'dp', 'tensor'), may hold values from -6 to 6
- attn_gain: bfloat16 [1024], P(('dp', 'seq')), may hold values from 0.099609375 to 1.8984375
- ffn_gain: bfloat16 [1024], P(('dp', 'seq')), may hold values from 0.099609375 to 1.8984375
- query_gain: bfloat16 [64], replicated, may hold values from 0.5 to 2.5
- key_gain: bfloat16 [64], replicated, may hold values from 0.5 to 2.5
- query_weight: bfloat16 [1024, 1024], P(('dp', 'seq'), 'tensor'), may hold values from -0.1875 to 0.1875
- key_weight: bfloat16 [1024, 512], P(('dp', 'seq'), 'tensor'), may hold values from -0.1875 to 0.1875
- value_weight: bfloat16 [1024, 512], P(('dp', 'seq'), 'tensor'), may hold values from -0.1875 to 0.1875
- out_weight: bfloat16 [1024, 1024], P(('dp', 'seq'), 'tensor'), may hold values from -2 to 2
- gate_weight: bfloat16 [1024, 4608], P(('dp', 'seq'), 'tensor'), may hold values from -0.1875 to 0.1875
- up_weight: bfloat16 [1024, 4608], P(('dp', 'seq'), 'tensor'), may hold values from -0.1875 to 0.1875
- down_weight: bfloat16 [1024, 4608], P(('dp', 'seq'), 'tensor'), may hold values from -0.09375 to 0.09375
- cotangent: bfloat16 [2048, 4, 1024], P('seq', 'dp', 'tensor'), may hold values from -6 to 6
Outputs:
- block_output: bfloat16 [2048, 4, 1024], P('seq', 'dp', 'tensor')
- input_grad: bfloat16 [2048, 4, 1024], P('seq', 'dp', 'tensor')
- attn_gain_grad: float32 [1024], P(('dp', 'seq'))
- ffn_gain_grad: float32 [1024], P(('dp', 'seq'))
- query_gain_grad: float32 [64], replicated
- key_gain_grad: float32 [64], replicated
- query_grad: float32 [1024, 1024], P(('dp', 'seq'), 'tensor')
- key_grad: float32 [1024, 512], P(('dp', 'seq'), 'tensor')
- value_grad: float32 [1024, 512], P(('dp', 'seq'), 'tensor')
- out_grad: float32 [1024, 1024], P(('dp', 'seq'), 'tensor')
- gate_grad: float32 [1024, 4608], P(('dp', 'seq'), 'tensor')
- up_grad: float32 [1024, 4608], P(('dp', 'seq'), 'tensor')
- down_grad: float32 [1024, 4608], P(('dp', 'seq'), 'tensor')
All inputs are finite; a program needn't handle non-finite values.
Results may differ from a plain program's by a relative error of at most 0.03.
Values may be sent and summed in bfloat16 or wider, within the bound.
No kernel may reach another device: no remote copies, remote signals or barrier semaphores. Data moves between devices by JAX's collectives and lax.ppermute only.
A program may use at most 64 MiB of HBM per device.

v0:
```python
import jax
import jax.numpy as jnp
from jax import lax
from jax.sharding import PartitionSpec as P

HD = 64
epsilon = 1e-05
rope_base = 1000000.0
far_below = -1e30


def rms_scale(values, gain):
    return values * lax.rsqrt(jnp.mean(values * values, axis=-1, keepdims=True) + epsilon) * gain


def swiglu(gate, up_part):
    return jax.nn.silu(gate) * up_part


def rotate(values, cosine, sine):
    half = values.shape[-1] // 2
    first = values[..., :half]
    second = values[..., half:]
    return jnp.concatenate(
        [first * cosine - second * sine, second * cosine + first * sine], axis=-1
    )


def project(left, right):
    return jnp.dot(left, right, preferred_element_type=jnp.float32)


def contract_rows(left, right):
    return lax.dot_general(
        left, right, (((0,), (0,)), ((), ())), preferred_element_type=jnp.float32
    )


def contract_cols(left, right):
    return lax.dot_general(
        left, right, (((1,), (1,)), ((), ())), preferred_element_type=jnp.float32
    )


def body(
    block_input,
    attn_gain,
    ffn_gain,
    query_gain,
    key_gain,
    query_weight,
    key_weight,
    value_weight,
    out_weight,
    gate_weight,
    up_weight,
    down_weight,
    cotangent,
):
    local_full = lax.all_gather(block_input, "tensor", axis=2, tiled=True)
    span, seq_local, width = local_full.shape
    row_count = span * seq_local
    feature_part = block_input.shape[2]
    feature_start = lax.axis_index("tensor") * feature_part
    seq_devices = lax.axis_size("seq")
    my_first = lax.axis_index("seq") * span
    kv_heads = key_weight.shape[1] // HD
    group = query_weight.shape[1] // key_weight.shape[1]
    kv_width = kv_heads * HD
    score_scale = HD ** (-0.5)
    gathered = (
        lax.all_gather(query_weight, ("dp", "seq"), axis=0, tiled=True),
        lax.all_gather(key_weight, ("dp", "seq"), axis=0, tiled=True),
        lax.all_gather(value_weight, ("dp", "seq"), axis=0, tiled=True),
        lax.all_gather(out_weight, ("dp", "seq"), axis=0, tiled=True),
        lax.all_gather(gate_weight, ("dp", "seq"), axis=0, tiled=True),
        lax.all_gather(up_weight, ("dp", "seq"), axis=0, tiled=True),
        lax.all_gather(down_weight, ("dp", "seq"), axis=0, tiled=True),
        lax.all_gather(attn_gain, ("dp", "seq"), axis=0, tiled=True),
        lax.all_gather(ffn_gain, ("dp", "seq"), axis=0, tiled=True),
    )
    (
        query_full,
        key_full,
        value_full,
        out_full,
        gate_full,
        up_full,
        down_full,
        gain_attn,
        gain_ffn,
    ) = gathered
    gain_one = gain_attn.astype(jnp.float32)
    gain_two = gain_ffn.astype(jnp.float32)
    head_query = query_gain.astype(jnp.float32)
    head_key = key_gain.astype(jnp.float32)
    positions = my_first + jnp.arange(span, dtype=jnp.int32)
    frequency = jnp.power(rope_base, -2.0 * jnp.arange(HD // 2, dtype=jnp.float32) / HD)
    angle = positions.astype(jnp.float32)[:, None] * frequency[None, :]
    cosine = jnp.cos(angle)[:, None, None, :]
    sine = jnp.sin(angle)[:, None, None, :]

    def shape_heads(raw, gain):
        heads = raw.reshape(span, seq_local, raw.shape[1] // HD, HD)
        return rotate(rms_scale(heads, gain), cosine, sine)

    base = local_full.reshape(row_count, width).astype(jnp.float32)
    normed_one = rms_scale(base, gain_one).astype(jnp.bfloat16)
    query_raw = project(normed_one, query_full)
    key_raw = project(normed_one, key_full)
    value_raw = project(normed_one, value_full)
    query_rot, pull_query = jax.vjp(shape_heads, query_raw, head_query)
    key_rot, pull_key = jax.vjp(shape_heads, key_raw, head_key)
    query_b = query_rot.astype(jnp.bfloat16).reshape(span, seq_local, kv_heads, group, HD)
    key_b = key_rot.astype(jnp.bfloat16).reshape(span, seq_local, kv_width)
    value_b = value_raw.astype(jnp.bfloat16).reshape(span, seq_local, kv_width)
    packed = jnp.concatenate([key_b, value_b], axis=-1)

    def split_piece(piece):
        count = piece.shape[0]
        return (
            piece[..., :kv_width].reshape(count, seq_local, kv_heads, HD),
            piece[..., kv_width:].reshape(count, seq_local, kv_heads, HD),
        )

    def scores_for(piece_keys):
        raw = (
            jnp.einsum("cskgd,pskd->cskgp", query_b, piece_keys, preferred_element_type=jnp.float32)
            * score_scale
        )
        key_pos = jnp.arange(piece_keys.shape[0], dtype=jnp.int32)
        allowed = (positions[:, None] >= key_pos[None, :])[:, None, None, None, :]
        return (raw, allowed)

    stat_shape = (span, seq_local, kv_heads, group)
    initial = (
        jnp.full(stat_shape, far_below, jnp.float32),
        jnp.zeros(stat_shape, jnp.float32),
        jnp.zeros(stat_shape + (HD,), jnp.float32),
    )
    piece = lax.all_gather(packed, "seq", axis=0, tiled=True)

    def forward_work(state):
        top, total, accum = state
        piece_keys, piece_values = split_piece(piece)
        raw, allowed = scores_for(piece_keys)
        new_top = jnp.maximum(top, jnp.max(jnp.where(allowed, raw, far_below), axis=-1))
        expo = jnp.where(allowed, jnp.exp(raw - new_top[..., None]), 0.0)
        total = jnp.sum(expo, axis=-1)
        accum = jnp.einsum(
            "cskgp,pskd->cskgd",
            expo.astype(jnp.bfloat16),
            piece_values,
            preferred_element_type=jnp.float32,
        )
        return (new_top, total, accum)

    top, total, accum = lax.cond(
        jnp.int32(0) <= my_first + span - 1, forward_work, lambda state: state, initial
    )
    attn_values = accum / total[..., None]
    log_total = top + jnp.log(total)
    attn_b = attn_values.reshape(row_count, -1).astype(jnp.bfloat16)
    attn_sum = lax.psum(contract_cols(attn_b, out_full).astype(jnp.bfloat16), "tensor").astype(
        jnp.float32
    )
    middle = base + attn_sum
    normed_two = rms_scale(middle, gain_two).astype(jnp.bfloat16)
    gate = project(normed_two, gate_full)
    up_part = project(normed_two, up_full)
    hidden = swiglu(gate, up_part).astype(jnp.bfloat16)
    ffn_mine = lax.psum_scatter(
        contract_cols(hidden, down_full).reshape(span, seq_local, width).astype(jnp.bfloat16),
        "tensor",
        scatter_dimension=2,
        tiled=True,
    ).astype(jnp.float32)
    middle_mine = lax.dynamic_slice_in_dim(
        middle.reshape(span, seq_local, width), feature_start, feature_part, 2
    )
    block_output = (middle_mine + ffn_mine).astype(jnp.bfloat16)
    again = (
        lax.all_gather(query_weight, ("dp", "seq"), axis=0, tiled=True),
        lax.all_gather(key_weight, ("dp", "seq"), axis=0, tiled=True),
        lax.all_gather(value_weight, ("dp", "seq"), axis=0, tiled=True),
        lax.all_gather(out_weight, ("dp", "seq"), axis=0, tiled=True),
        lax.all_gather(gate_weight, ("dp", "seq"), axis=0, tiled=True),
        lax.all_gather(up_weight, ("dp", "seq"), axis=0, tiled=True),
        lax.all_gather(down_weight, ("dp", "seq"), axis=0, tiled=True),
    )
    query_back, key_back, value_back, out_back, gate_back, up_back, down_back = again
    cot_full = lax.all_gather(cotangent, "tensor", axis=2, tiled=True).reshape(row_count, width)
    hidden_grad = project(cot_full, down_back)
    down_sum = contract_rows(cot_full, hidden)
    _, pull_swiglu = jax.vjp(swiglu, gate, up_part)
    gate_grad, up_grad = pull_swiglu(hidden_grad)
    gate_gb = gate_grad.astype(jnp.bfloat16)
    up_gb = up_grad.astype(jnp.bfloat16)
    normed_two_grad = lax.psum(
        (contract_cols(gate_gb, gate_back) + contract_cols(up_gb, up_back)).astype(jnp.bfloat16),
        "tensor",
    ).astype(jnp.float32)
    gate_sum = contract_rows(normed_two, gate_gb)
    up_sum = contract_rows(normed_two, up_gb)
    _, pull_two = jax.vjp(rms_scale, middle, gain_two)
    middle_norm_grad, gain_two_grad = pull_two(normed_two_grad)
    middle_grad = cot_full.astype(jnp.float32) + middle_norm_grad
    middle_gb = middle_grad.astype(jnp.bfloat16)
    attn_grad = project(middle_gb, out_back)
    out_sum = contract_rows(middle_gb, attn_b)
    attn_full = attn_grad.reshape(span, seq_local, kv_heads, group, HD)
    attn_gb = attn_full.astype(jnp.bfloat16)
    delta = jnp.sum(attn_full * attn_values, axis=-1)
    full_length = span * seq_devices
    back_initial = (
        jnp.zeros(stat_shape + (HD,), jnp.float32),
        jnp.zeros((full_length, seq_local, 2 * kv_width), jnp.float32),
    )
    backward_piece = lax.all_gather(packed, "seq", axis=0, tiled=True)

    def backward_work(state):
        piece_keys, piece_values = split_piece(backward_piece)
        raw, allowed = scores_for(piece_keys)
        probs = jnp.where(allowed, jnp.exp(raw - log_total[..., None]), 0.0)
        prob_grad = jnp.einsum(
            "cskgd,pskd->cskgp", attn_gb, piece_values, preferred_element_type=jnp.float32
        )
        score_gb = (probs * (prob_grad - delta[..., None])).astype(jnp.bfloat16)
        query_acc = (
            jnp.einsum(
                "cskgp,pskd->cskgd", score_gb, piece_keys, preferred_element_type=jnp.float32
            )
            * score_scale
        )
        key_part = (
            jnp.einsum("cskgp,cskgd->pskd", score_gb, query_b, preferred_element_type=jnp.float32)
            * score_scale
        )
        value_part = jnp.einsum(
            "cskgp,cskgd->pskd",
            probs.astype(jnp.bfloat16),
            attn_gb,
            preferred_element_type=jnp.float32,
        )
        count = backward_piece.shape[0]
        term = jnp.concatenate(
            [
                key_part.reshape(count, seq_local, kv_width),
                value_part.reshape(count, seq_local, kv_width),
            ],
            axis=-1,
        )
        return (query_acc, term)

    query_hgrad, kv_total = lax.cond(
        jnp.int32(0) <= my_first + span - 1, backward_work, lambda state: state, back_initial
    )
    kv_mine = lax.psum_scatter(
        kv_total.astype(jnp.bfloat16), "seq", scatter_dimension=0, tiled=True
    ).astype(jnp.float32)
    query_raw_grad, query_gain_part = pull_query(
        query_hgrad.reshape(span, seq_local, kv_heads * group, HD)
    )
    key_raw_grad, key_gain_part = pull_key(
        kv_mine[..., :kv_width].reshape(span, seq_local, kv_heads, HD)
    )
    query_gb = query_raw_grad.astype(jnp.bfloat16)
    key_gb = key_raw_grad.astype(jnp.bfloat16)
    value_gb = kv_mine[..., kv_width:].reshape(row_count, kv_width).astype(jnp.bfloat16)
    normed_one_grad = lax.psum(
        (
            contract_cols(query_gb, query_back)
            + contract_cols(key_gb, key_back)
            + contract_cols(value_gb, value_back)
        ).astype(jnp.bfloat16),
        "tensor",
    ).astype(jnp.float32)
    query_sum = contract_rows(normed_one, query_gb)
    key_sum = contract_rows(normed_one, key_gb)
    value_sum = contract_rows(normed_one, value_gb)
    _, pull_one = jax.vjp(rms_scale, base, gain_one)
    base_norm_grad, gain_one_grad = pull_one(normed_one_grad)
    input_full = (middle_grad + base_norm_grad).reshape(span, seq_local, width)
    input_grad = lax.dynamic_slice_in_dim(input_full, feature_start, feature_part, 2).astype(
        jnp.bfloat16
    )
    summed = (
        lax.psum_scatter(
            gain_one_grad.astype(jnp.bfloat16), ("dp", "seq"), scatter_dimension=0, tiled=True
        ).astype(jnp.float32),
        lax.psum_scatter(
            gain_two_grad.astype(jnp.bfloat16), ("dp", "seq"), scatter_dimension=0, tiled=True
        ).astype(jnp.float32),
        lax.psum_scatter(
            query_sum.astype(jnp.bfloat16), ("dp", "seq"), scatter_dimension=0, tiled=True
        ).astype(jnp.float32),
        lax.psum_scatter(
            key_sum.astype(jnp.bfloat16), ("dp", "seq"), scatter_dimension=0, tiled=True
        ).astype(jnp.float32),
        lax.psum_scatter(
            value_sum.astype(jnp.bfloat16), ("dp", "seq"), scatter_dimension=0, tiled=True
        ).astype(jnp.float32),
        lax.psum_scatter(
            out_sum.astype(jnp.bfloat16), ("dp", "seq"), scatter_dimension=0, tiled=True
        ).astype(jnp.float32),
        lax.psum_scatter(
            gate_sum.astype(jnp.bfloat16), ("dp", "seq"), scatter_dimension=0, tiled=True
        ).astype(jnp.float32),
        lax.psum_scatter(
            up_sum.astype(jnp.bfloat16), ("dp", "seq"), scatter_dimension=0, tiled=True
        ).astype(jnp.float32),
        lax.psum_scatter(
            down_sum.astype(jnp.bfloat16), ("dp", "seq"), scatter_dimension=0, tiled=True
        ).astype(jnp.float32),
    )
    head_sums = lax.psum((query_gain_part, key_gain_part), ("dp", "seq", "tensor"))
    return (
        block_output,
        input_grad,
        summed[0],
        summed[1],
        head_sums[0],
        head_sums[1],
        summed[2],
        summed[3],
        summed[4],
        summed[5],
        summed[6],
        summed[7],
        summed[8],
    )


def solution(mesh):
    return jax.shard_map(
        body,
        mesh=mesh,
        in_specs=(
            P("seq", "dp", "tensor"),
            P(("dp", "seq")),
            P(("dp", "seq")),
            P(),
            P(),
            P(("dp", "seq"), "tensor"),
            P(("dp", "seq"), "tensor"),
            P(("dp", "seq"), "tensor"),
            P(("dp", "seq"), "tensor"),
            P(("dp", "seq"), "tensor"),
            P(("dp", "seq"), "tensor"),
            P(("dp", "seq"), "tensor"),
            P("seq", "dp", "tensor"),
        ),
        out_specs=(
            P("seq", "dp", "tensor"),
            P("seq", "dp", "tensor"),
            P(("dp", "seq")),
            P(("dp", "seq")),
            P(),
            P(),
            P(("dp", "seq"), "tensor"),
            P(("dp", "seq"), "tensor"),
            P(("dp", "seq"), "tensor"),
            P(("dp", "seq"), "tensor"),
            P(("dp", "seq"), "tensor"),
            P(("dp", "seq"), "tensor"),
            P(("dp", "seq"), "tensor"),
        ),
        check_vma=False,
    )
```

profile of v0, /device:TPU:0, one launch (start us, length us, event | category | flops | bytes accessed | tf_op | source)
XLA Modules:
  0.0 1089.4 jit_solution(527268343555547212)
XLA Ops:
  12.4 68.5 %all-reduce.10 = (bf16[1024]{0:T(1024)(128)(2,1)S(1)}, bf16[1024]{0:T(1024)(128)(2,1)S(1)}) all-reduce(bf16[1024]{0:T(1024)(128)(2,1)S(1)} %dynamic-update-slice.1, bf16[1024]{0:T(1024)(128)(2,1)S(1)} %dynamic-update-slice), channel_id=1, replica_groups=mesh['dp'=4,'seq'=8,'tensor'=4] {'dp','seq'}, use_global_device_ids=true, to_apply=%add.5 | all-reduce | flops 2048 | bytes 8192
  80.9 22.4 %all_gather.46 = bf16[1024,128]{1,0:T(8,128)(2,1)S(1)} all-gather(bf16[32,128]{1,0:T(8,128)(2,1)} %param.23), channel_id=1, replica_groups=mesh['dp'=4,'seq'=8,'tensor'=4] {'dp','seq'}, dimensions={0}, use_global_device_ids=true | all-gather | bytes 270336 | tf_op jit(solution)/shard_map/all_gather | solution.py:73
  103.3 24.3 %all_gather.47 = bf16[1024,128]{1,0:T(8,128)(2,1)S(1)} all-gather(bf16[32,128]{1,0:T(8,128)(2,1)} %param.24), channel_id=1, replica_groups=mesh['dp'=4,'seq'=8,'tensor'=4] {'dp','seq'}, dimensions={0}, use_global_device_ids=true | all-gather | bytes 270336 | tf_op jit(solution)/shard_map/all_gather | solution.py:74
  127.6 13.7 %all_gather.44 = bf16[256,1,1024]{2,0,1:T(8,128)(2,1)S(1)} all-gather(bf16[256,1,256]{2,0,1:T(8,128)(2,1)} %param.17), channel_id=1, replica_groups=mesh['dp'=4,'seq'=8,'tensor'=4] {'tensor'}, dimensions={2}, use_global_device_ids=true | all-gather | bytes 655360 | tf_op jit(solution)/shard_map/all_gather | solution.py:60
  145.0 22.4 %all_gather.49 = bf16[1024,256]{1,0:T(8,128)(2,1)S(1)} all-gather(bf16[32,256]{1,0:T(8,128)(2,1)S(1)} %copy-done.34), channel_id=1, replica_groups=mesh['dp'=4,'seq'=8,'tensor'=4] {'dp','seq'}, dimensions={0}, use_global_device_ids=true | all-gather | bytes 540672 | tf_op jit(solution)/shard_map/all_gather | solution.py:72
  168.9 24.4 %all_gather.50 = bf16[1024,256]{1,0:T(8,128)(2,1)S(1)} all-gather(bf16[32,256]{1,0:T(8,128)(2,1)S(1)} %copy-done.35), channel_id=1, replica_groups=mesh['dp'=4,'seq'=8,'tensor'=4] {'dp','seq'}, dimensions={0}, use_global_device_ids=true | all-gather | bytes 540672 | tf_op jit(solution)/shard_map/all_gather | solution.py:75
  193.3 8.4 conditional.2
  195.6 2.4 fusion
  198.1 1.8 fusion.9
  199.9 1.8 fusion.4
  205.5 14.8 %all_gather.55 = bf16[256,1,1024]{2,0,1:T(8,128)(2,1)S(1)} all-gather(bf16[256,1,256]{2,0,1:T(8,128)(2,1)S(1)} %copy-done.27), channel_id=1, replica_groups=mesh['dp'=4,'seq'=8,'tensor'=4] {'tensor'}, dimensions={2}, use_global_device_ids=true | all-gather | bytes 655360 | tf_op jit(solution)/shard_map/all_gather | solution.py:192
  220.2 25.8 %all-reduce.15.cloned.1.call-done = bf16[256,1024]{1,0:T(8,128)(2,1)} async-done(((bf16[256,1024]{1,0:T(8,128)(2,1)}), bf16[256,1024]{1,0:T(8,128)(2,1)}) %all-reduce.15.cloned.1.call-update) | async-done | bytes 524304 | tf_op jit(solution)/shard_map/psum | solution.py:164
  249.3 3.6 fusion.106
  252.9 42.1 %all-gather.7.cloned.1.call-done = bf16[1024,1152]{1,0:T(8,128)(2,1)} async-done(((bf16[32,1152]{1,0:T(8,128)(2,1)}), bf16[1024,1152]{1,0:T(8,128)(2,1)}) %all-gather.7.cloned.1.call-update) | async-done | bytes 2359312 | tf_op jit(solution)/shard_map/all_gather | solution.py:76
  295.0 3.6 fusion.105
  298.6 42.1 %all-gather.11.cloned.1.call-done = bf16[1024,1152]{1,0:T(8,128)(2,1)} async-done(((bf16[32,1152]{1,0:T(8,128)(2,1)}), bf16[1024,1152]{1,0:T(8,128)(2,1)}) %all-gather.11.cloned.1.call-update) | async-done | bytes 2359312 | tf_op jit(solution)/shard_map/all_gather | solution.py:78
  340.7 4.4 multiply_convert_fusion
  349.2 42.2 %all-reduce.17.cloned.1.call-done = bf16[256,1024]{1,0:T(8,128)(2,1)} async-done(((bf16[256,1024]{1,0:T(8,128)(2,1)}), bf16[256,1024]{1,0:T(8,128)(2,1)}) %all-reduce.17.cloned.1.call-update) | async-done | bytes 524304 | tf_op jit(solution)/shard_map/psum | solution.py:199
  391.4 2.1 fusion.57
  394.2 2.5 fusion.69
  397.1 15.4 %conditional.3 = (bf16[2048,1,256]{0,2,1:T(8,128)(2,1)}, f32[256,1,4,32]{0,3,2,1:T(8,128)S(1)}, f32[256,1,4,32]{0,3,2,1:T(8,128)S(1)}, f32[256,1,4,32]{0,3,2,1:T(8,128)S(1)}) conditional(s32[]{:T(128)} %convert_element_type.243, () %tuple.37, (s32[256]{0:T(256)}, bf16[2048,1,256]{0,2,1:T(8,128)(2,1)}, bf16[256,1,2,2,64]{0,4,3,2,1:T(8,128)(2,1)}, ...), branch_computations={%region_12.13_spmd, %region_13.15_spmd} | conditional | flops 1366589440 | bytes 49067068 | solution.py:255
  401.2 2.2 fusion.40
  403.4 1.9 fusion.27
  405.3 2.9 fusion.18
  409.0 2.3 fusion.33
  413.2 3.5 fusion.50
  421.4 24.7 %reduce-scatter.14.cloned.1.call-done = bf16[256,1,256]{0,2,1:T(8,128)(2,1)} async-done(((bf16[2048,1,256]{0,2,1:T(8,128)(2,1)}), bf16[256,1,256]{0,2,1:T(8,128)(2,1)}) %reduce-scatter.14.cloned.1.call-update) | async-done | bytes 131088 | tf_op jit(solution)/shard_map/reduce_scatter | solution.py:258
  449.0 1.8 convolution_convert_fusion.8
  450.9 2.1 convolution_convert_fusion.7
  453.0 2.3 fusion.108
  456.5 2.4 fusion.46
  459.1 3.3 fusion.44
  462.4 4.3 copy.50
  467.7 2.3 convolution_convert_fusion.1
  470.2 2.4 convolution_convert_fusion.2
  473.4 1.7 fusion.77
  475.1 73.5 %reduce-scatter.22.cloned.1.call-done = bf16[32,256]{1,0:T(8,128)(2,1)} async-done(((bf16[1024,256]{1,0:T(8,128)(2,1)}), bf16[32,256]{1,0:T(8,128)(2,1)}) %reduce-scatter.22.cloned.1.call-update) | async-done | bytes 16400 | tf_op jit(solution)/shard_map/reduce_scatter | solution.py:303
  549.9 78.5 %reduce-scatter.16.cloned.1.call-done = bf16[32,256]{1,0:T(8,128)(2,1)} async-done(((bf16[1024,256]{1,0:T(8,128)(2,1)}), bf16[32,256]{1,0:T(8,128)(2,1)}) %reduce-scatter.16.cloned.1.call-update) | async-done | bytes 16400 | tf_op jit(solution)/shard_map/reduce_scatter | solution.py:294
  629.8 64.6 %all-reduce.8 = (f32[64]{0:T(128)}, f32[64]{0:T(128)}) all-reduce(f32[64]{0:T(128)S(1)} %copy-done.52, f32[64]{0:T(128)S(1)} %copy-done.51), channel_id=1, replica_groups=mesh['dp'=4,'seq'=8,'tensor'=4] {'dp','seq','tensor'}, use_global_device_ids=true, to_apply=%region_25.26 | all-reduce | flops 128 | bytes 1024 | tf_op jit(solution)/shard_map/psum | solution.py:316
  694.4 13.8 %reduce-scatter.18.cloned.1.call-done = bf16[32,128]{1,0:T(8,128)(2,1)} async-done(((bf16[1024,128]{1,0:T(8,128)(2,1)}), bf16[32,128]{1,0:T(8,128)(2,1)}) %reduce-scatter.18.cloned.1.call-update) | async-done | bytes 8208 | tf_op jit(solution)/shard_map/reduce_scatter | solution.py:297
  709.4 78.4 %reduce-scatter.20.cloned.1.call-done = bf16[32,128]{1,0:T(8,128)(2,1)} async-done(((bf16[1024,128]{1,0:T(8,128)(2,1)}), bf16[32,128]{1,0:T(8,128)(2,1)}) %reduce-scatter.20.cloned.1.call-update) | async-done | bytes 8208 | tf_op jit(solution)/shard_map/reduce_scatter | solution.py:300
  789.2 43.1 %all-reduce.19.cloned.1.call-done = bf16[256,1024]{1,0:T(8,128)(2,1)} async-done(((bf16[256,1024]{1,0:T(8,128)(2,1)}), bf16[256,1024]{1,0:T(8,128)(2,1)}) %all-reduce.19.cloned.1.call-update) | async-done | bytes 524304 | tf_op jit(solution)/shard_map/psum | solution.py:270
  832.2 2.5 fusion.58
  834.7 65.3 %all-reduce.9 = (bf16[1024]{0:T(1024)(128)(2,1)S(1)}, bf16[1024]{0:T(1024)(128)(2,1)S(1)}) all-reduce(bf16[1024]{0:T(1024)(128)(2,1)S(1)} %get-tuple-element.145, bf16[1024]{0:T(1024)(128)(2,1)S(1)} %copy-done.45), channel_id=4, replica_groups=mesh['dp'=4,'seq'=8,'tensor'=4] {'dp','seq'}, use_global_device_ids=true, to_apply=%region_21.22.clone | all-reduce | flops 2048 | bytes 8192
  900.6 1.8 fusion.82
  902.4 13.4 %reduce-scatter.28.cloned.1.call-done = bf16[32,1152]{1,0:T(8,128)(2,1)} async-done(((bf16[1024,1152]{1,0:T(8,128)(2,1)}), bf16[32,1152]{1,0:T(8,128)(2,1)}) %reduce-scatter.28.cloned.1.call-update) | async-done | bytes 73744
  917.7 80.6 %reduce-scatter.26.cloned.1.call-done = bf16[32,1152]{1,0:T(8,128)(2,1)} async-done(((bf16[1024,1152]{1,0:T(8,128)(2,1)}), bf16[32,1152]{1,0:T(8,128)(2,1)}) %reduce-scatter.26.cloned.1.call-update) | async-done | bytes 73744 | tf_op jit(solution)/shard_map/reduce_scatter | solution.py:309
  999.8 80.7 %reduce-scatter.24.cloned.1.call-done = bf16[32,1152]{1,0:T(8,128)(2,1)} async-done(((bf16[1024,1152]{1,0:T(8,128)(2,1)}), bf16[32,1152]{1,0:T(8,128)(2,1)}) %reduce-scatter.24.cloned.1.call-update) | async-done | bytes 73744 | tf_op jit(solution)/shard_map/reduce_scatter | solution.py:306
  (216 shorter events, 50.6 us)
Async XLA Ops:
  8.0 185.3 %all-gather.5.cloned.1.call-start = ((), (), s32[]{:S(2)}) async-start(), calls=%async_computation.9 | async-start | bytes 1179648 | tf_op jit(solution)/shard_map/all_gather | solution.py:141
  8.8 134.5 %copy-start.46 = (f32[64]{0:T(128)}, f32[64]{0:T(128)S(1)}, u32[]{:S(2)}) copy-start(f32[64]{0:T(128)S(1)} %convert_element_type.246) | copy-start | bytes 772
  80.9 86.5 %copy-start.32 = (f32[1024]{0:T(1024)}, f32[1024]{0:T(1024)S(1)}, u32[]{:S(2)}) copy-start(f32[1024]{0:T(1024)S(1)} %convert_element_type.244) | copy-start | bytes 12292
  103.3 40.9 %copy-start.15 = (bf16[1024,128]{1,0:T(8,128)(2,1)}, bf16[1024,128]{1,0:T(8,128)(2,1)S(1)}, u32[]{:S(2)}) copy-start(bf16[1024,128]{1,0:T(8,128)(2,1)S(1)} %all_gather.46) | copy-start | bytes 786436
  127.6 16.8 %copy-start.13 = (bf16[1024,128]{1,0:T(8,128)(2,1)}, bf16[1024,128]{1,0:T(8,128)(2,1)S(1)}, u32[]{:S(2)}) copy-start(bf16[1024,128]{1,0:T(8,128)(2,1)S(1)} %all_gather.47) | copy-start | bytes 786436
  127.6 16.8 %copy-start.53 = (bf16[64]{0:T(256)(128)(2,1)S(1)}, bf16[64]{0:T(256)(128)(2,1)}, u32[]{:S(2)}) copy-start(bf16[64]{0:T(256)(128)(2,1)} %param.20) | copy-start | bytes 388
  127.6 17.4 %copy-start.34 = (bf16[32,256]{1,0:T(8,128)(2,1)S(1)}, bf16[32,256]{1,0:T(8,128)(2,1)}, u32[]{:S(2)}) copy-start(bf16[32,256]{1,0:T(8,128)(2,1)} %param.22) | copy-start | bytes 49156
  142.1 25.7 %copy-start.39 = (f32[256]{0:T(256)}, f32[256]{0:T(256)S(1)}, u32[]{:S(2)}) copy-start(f32[256]{0:T(256)S(1)} %fusion.89) | copy-start | bytes 3076
  142.9 25.9 %copy-start.35 = (bf16[32,256]{1,0:T(8,128)(2,1)S(1)}, bf16[32,256]{1,0:T(8,128)(2,1)}, u32[]{:S(2)}) copy-start(bf16[32,256]{1,0:T(8,128)(2,1)} %param.25) | copy-start | bytes 49156
  143.2 50.1 %copy-start.16 = (f32[256,32]{0,1:T(8,128)}, f32[256,32]{0,1:T(8,128)S(1)}, u32[]{:S(2)}) copy-start(f32[256,32]{0,1:T(8,128)S(1)} %get-tuple-element.184) | copy-start | bytes 98308
  143.2 50.1 %copy-start.18 = (f32[256,32]{0,1:T(8,128)}, f32[256,32]{0,1:T(8,128)S(1)}, u32[]{:S(2)}) copy-start(f32[256,32]{0,1:T(8,128)S(1)} %get-tuple-element.185) | copy-start | bytes 98308
  144.3 101.8 %all-reduce.15.cloned.1.call-start = ((), (), s32[]{:S(2)}) async-start(), calls=%async_computation.10 | async-start | bytes 1048576 | tf_op jit(solution)/shard_map/psum | solution.py:164
  144.4 48.9 %copy-start.48 = (f32[64]{0:T(128)}, f32[64]{0:T(128)S(1)}, u32[]{:S(2)}) copy-start(f32[64]{0:T(128)S(1)} %convert_element_type.250) | copy-start | bytes 772
  193.3 9.2 copy-start.3
  201.7 3.7 copy-start.36
  201.7 3.8 copy-start.27
  202.5 46.2 %copy-start.11 = (bf16[256,1,2,2,64]{0,4,3,2,1:T(8,128)(2,1)}, bf16[256,1,2,2,64]{0,4,3,2,1:T(8,128)(2,1)S(1)}, u32[]{:S(2)}) copy-start(bf16[256,1,2,2,64]{0,4,3,2,1:T(8,128)(2,1)S(1)} %get-tuple-element.159) | copy-start | bytes 393220
  203.6 45.6 %all-gather.9.cloned.1.call-start = ((), (), s32[]{:S(2)}) async-start(), calls=%async_computation.12 | async-start | bytes 2433024 | tf_op jit(solution)/shard_map/all_gather | solution.py:77
  204.2 90.8 %all-gather.7.cloned.1.call-start = ((), (), s32[]{:S(2)}) async-start(), calls=%async_computation.11 | async-start | bytes 2433024 | tf_op jit(solution)/shard_map/all_gather | solution.py:76
  204.8 135.9 %all-gather.11.cloned.1.call-start = ((), (), s32[]{:S(2)}) async-start(), calls=%async_computation.13 | async-start | bytes 2433024 | tf_op jit(solution)/shard_map/all_gather | solution.py:78
  205.4 186.0 %all-reduce.17.cloned.1.call-start = ((), (), s32[]{:S(2)}) async-start(), calls=%async_computation.15 | async-start | bytes 1048576 | tf_op jit(solution)/shard_map/psum | solution.py:199
  247.3 5.5 copy-start.44
  247.4 5.5 copy-start.38
  340.7 4.4 copy-start.1
  347.2 44.1 %copy-start.2 = (bf16[256,1024]{1,0:T(8,128)(2,1)S(1)}, bf16[256,1024]{1,0:T(8,128)(2,1)}, u32[]{:S(2)}) copy-start(bf16[256,1024]{1,0:T(8,128)(2,1)} %all-reduce.15.cloned.1.call-done) | copy-start | bytes 1572868
  348.9 97.1 %reduce-scatter.14.cloned.1.call-start = ((), (), s32[]{:S(2)}) async-start(), calls=%async_computation.16 | async-start | bytes 1179648 | tf_op jit(solution)/shard_map/reduce_scatter | solution.py:258
  412.5 4.3 copy-start.24
  413.2 60.2 %reduce-scatter.12.cloned.1.call-start = ((), (), s32[]{:S(2)}) async-start(), calls=%async_computation.14 | async-start | bytes 655360 | tf_op jit(solution)/shard_map/reduce_scatter | solution.py:172
  416.9 131.7 %reduce-scatter.22.cloned.1.call-start = ((), (), s32[]{:S(2)}) async-start(), calls=%async_computation.21 | async-start | bytes 540672 | tf_op jit(solution)/shard_map/reduce_scatter | solution.py:303
  418.1 28.9 %copy-start.29 = (f32[256,2]{0,1:T(2,128)S(1)}, f32[256,2]{0,1:T(2,128)}, u32[]{:S(2)}) copy-start(f32[256,2]{0,1:T(2,128)} %copy-done.28) | copy-start | bytes 6148
  418.1 28.9 %copy-start.47 = (f32[64]{0:T(128)S(1)}, f32[64]{0:T(128)}, u32[]{:S(2)}) copy-start(f32[64]{0:T(128)} %copy-done.46) | copy-start | bytes 772
  418.1 29.5 %copy-start.31 = (f32[256,2]{0,1:T(2,128)S(1)}, f32[256,2]{0,1:T(2,128)}, u32[]{:S(2)}) copy-start(f32[256,2]{0,1:T(2,128)} %copy-done.30) | copy-start | bytes 6148
  418.1 210.3 %reduce-scatter.16.cloned.1.call-start = ((), (), s32[]{:S(2)}) async-start(), calls=%async_computation.18 | async-start | bytes 540672 | tf_op jit(solution)/shard_map/reduce_scatter | solution.py:294
  420.0 26.9 %copy-start.20 = (bf16[256,1,4,64]{0,3,2,1:T(8,128)(2,1)}, bf16[256,1,4,64]{0,3,2,1:T(8,128)(2,1)S(1)}, u32[]{:S(2)}) copy-start(bf16[256,1,4,64]{0,3,2,1:T(8,128)(2,1)S(1)} %fusion.74) | copy-start | bytes 393220
  420.0 30.9 %copy-start.41 = (f32[256]{0:T(256)S(1)}, f32[256]{0:T(256)}, u32[]{:S(2)}) copy-start(f32[256]{0:T(256)} %copy-done.39) | copy-start | bytes 3076
  421.4 286.8 %reduce-scatter.18.cloned.1.call-start = ((), (), s32[]{:S(2)}) async-start(), calls=%async_computation.19 | async-start | bytes 270336 | tf_op jit(solution)/shard_map/reduce_scatter | solution.py:297
  447.0 8.4 copy-start.14
  450.9 5.7 copy-start.10
  450.9 5.7 copy-start.21
  450.9 337.0 %reduce-scatter.20.cloned.1.call-start = ((), (), s32[]{:S(2)}) async-start(), calls=%async_computation.20 | async-start | bytes 270336 | tf_op jit(solution)/shard_map/reduce_scatter | solution.py:300
  455.3 376.9 %all-reduce.19.cloned.1.call-start = ((), (), s32[]{:S(2)}) async-start(), calls=%async_computation.17 | async-start | bytes 1048576 | tf_op jit(solution)/shard_map/psum | solution.py:270
  459.0 456.8 %reduce-scatter.28.cloned.1.call-start = ((), (), s32[]{:S(2)}) async-start(), calls=%async_computation.24 | async-start | bytes 2433024
  466.7 531.6 %reduce-scatter.26.cloned.1.call-start = ((), (), s32[]{:S(2)}) async-start(), calls=%async_computation.23 | async-start | bytes 2433024 | tf_op jit(solution)/shard_map/reduce_scatter | solution.py:309
  470.1 610.4 %reduce-scatter.24.cloned.1.call-start = ((), (), s32[]{:S(2)}) async-start(), calls=%async_computation.22 | async-start | bytes 2433024 | tf_op jit(solution)/shard_map/reduce_scatter | solution.py:306
  472.5 157.3 %copy-start.51 = (f32[64]{0:T(128)S(1)}, f32[64]{0:T(128)}, u32[]{:S(2)}) copy-start(f32[64]{0:T(128)} %get-tuple-element.149) | copy-start | bytes 772
  472.5 157.3 %copy-start.52 = (f32[64]{0:T(128)S(1)}, f32[64]{0:T(128)}, u32[]{:S(2)}) copy-start(f32[64]{0:T(128)} %get-tuple-element.147) | copy-start | bytes 772
  472.5 362.2 %copy-start.45 = (bf16[1024]{0:T(1024)(128)(2,1)S(1)}, bf16[1024]{0:T(1024)(128)(2,1)}, u32[]{:S(2)}) copy-start(bf16[1024]{0:T(1024)(128)(2,1)} %get-tuple-element.143) | copy-start | bytes 6148
  472.5 428.1 %copy-start.43 = (f32[256]{0:T(256)S(1)}, f32[256]{0:T(256)}, u32[]{:S(2)}) copy-start(f32[256]{0:T(256)} %copy-done.42) | copy-start | bytes 3076
  (22 other events, 38.1 us)
Sparse Core Ops, SparseCore 0:
  144.4 22.6 all-gather.4
  203.8 42.2 all-reduce.14
  349.1 42.2 all-reduce.16
  413.3 32.7 reduce-scatter.13
  448.3 20.0 reduce-scatter.11
  471.7 76.8 reduce-scatter.21
  552.0 76.3 reduce-scatter.15
  631.9 76.2 reduce-scatter.17
  711.6 76.2 reduce-scatter.19
  790.0 42.1 all-reduce.18
  835.8 79.9 reduce-scatter.27
  919.6 78.6 reduce-scatter.25
  1001.9 78.5 reduce-scatter.23
Sparse Core Ops, SparseCore 1:
  206.4 42.8 all-gather.8
  251.4 43.6 all-gather.6
  297.1 43.6 all-gather.10
where the time goes:
time: 1090 us
  waiting for transfers between devices  641 us (59%)
  blocking collectives  320 us (29%)
  matrix products  55 us (5%)
  other arithmetic  36.8 us (3%)
  between operations  17.6 us (2%)
  local copies, waits for them, and re-layouts  17.2 us (2%)
    unnamed x2, blocking collectives  134 us
    reduce_scatter x1, waiting for transfers between devices, body(): lax.psum_scatter(gate_sum.astype(jnp.bfloat16), ('dp', 'seq'), scatter_di...  80.7 us
    reduce_scatter x1, waiting for transfers between devices, body(): lax.psum_scatter(up_sum.astype(jnp.bfloat16), ('dp', 'seq'), scatter_dime...  80.6 us
    reduce_scatter x1, waiting for transfers between devices, body(): lax.psum_scatter(query_sum.astype(jnp.bfloat16), ('dp', 'seq'), scatter_d...  78.5 us
    reduce_scatter x1, waiting for transfers between devices, body(): lax.psum_scatter(value_sum.astype(jnp.bfloat16), ('dp', 'seq'), scatter_d...  78.4 us
    reduce_scatter x1, waiting for transfers between devices, body(): lax.psum_scatter(out_sum.astype(jnp.bfloat16), ('dp', 'seq'), scatter_dim...  73.5 us
    psum x1, blocking collectives, body(): lax.psum((query_gain_part, key_gain_part), ('dp', 'seq', 'tensor'))  64.6 us
    psum x1, waiting for transfers between devices, body(): lax.psum((contract_cols(query_gb, query_back) + contract_cols(key_gb, key...  43.1 us
  transfers between devices with their start and end apart: 16, of which 14 were waited for; matrix products, arithmetic and copies ran while one was open for 5% of the time, Pallas kernels for 0%

commit v1 on v0

--- a/solution.py
+++ b/solution.py
@@ -7,6 +7,12 @@
 epsilon = 1e-05
 rope_base = 1000000.0
 far_below = -1e30
+
+
+def summed_here(x, axis):
+    terms = lax.all_gather(x, axis, axis=0, tiled=False)
+    summed = terms.sum(axis=0)
+    return summed
 
 
 def rms_scale(values, gain):
@@ -267,7 +273,7 @@
     query_gb = query_raw_grad.astype(jnp.bfloat16)
     key_gb = key_raw_grad.astype(jnp.bfloat16)
     value_gb = kv_mine[..., kv_width:].reshape(row_count, kv_width).astype(jnp.bfloat16)
-    normed_one_grad = lax.psum(
+    normed_one_grad = summed_here(
         (
             contract_cols(query_gb, query_back)
             + contract_cols(key_gb, key_back)

time: 1090 us -> 1140 us (1.046)
  waiting for transfers between devices: 641 us -> 702 us
    unnamed x17, waiting for transfers between devices: 15.2 us -> 82.6 us
    psum x1 -> x0, waiting for transfers between devices: 43.1 us -> none  [body(): lax.psum((contract_cols(query_gb, query_back) + contract_cols(key_gb, key...]
    all_gather x1, waiting for transfers between devices: 42.1 us -> 0.56 us  [body(): lax.all_gather(gate_weight, ('dp', 'seq'), axis=0, tiled=True)]
    all_gather x1, waiting for transfers between devices: 0.59 us -> 42.1 us  [body(): lax.all_gather(up_weight, ('dp', 'seq'), axis=0, tiled=True)]
    all_gather x0 -> x1, waiting for transfers between devices: none -> 30.4 us  [summed_here(): terms = lax.all_gather(x, axis, axis=0, tiled=False)]
  transfers between devices with their start and end apart: 16 -> 16, of which waited for: 14 -> 15; matrix products, arithmetic and copies ran while one was open for 5% -> 4% of each run, Pallas kernels for 0% -> 0%
where the time goes in v1:
time: 1140 us
  waiting for transfers between devices  702 us (62%)
  blocking collectives  318 us (28%)
  matrix products  49.2 us (4%)
  other arithmetic  34.9 us (3%)
  local copies, waits for them, and re-layouts  18.6 us (2%)
  between operations  17.6 us (2%)
    unnamed x2, blocking collectives  131 us
    unnamed x17, waiting for transfers between devices  82.6 us
    reduce_scatter x1, waiting for transfers between devices, body(): lax.psum_scatter(gate_sum.astype(jnp.bfloat16), ('dp', 'seq'), scatter_di...  80.7 us
    reduce_scatter x1, waiting for transfers between devices, body(): lax.psum_scatter(up_sum.astype(jnp.bfloat16), ('dp', 'seq'), scatter_dime...  80.5 us
    reduce_scatter x1, waiting for transfers between devices, body(): lax.psum_scatter(query_sum.astype(jnp.bfloat16), ('dp', 'seq'), scatter_d...  78.5 us
    reduce_scatter x1, waiting for transfers between devices, body(): lax.psum_scatter(out_sum.astype(jnp.bfloat16), ('dp', 'seq'), scatter_dim...  78.5 us
    reduce_scatter x1, waiting for transfers between devices, body(): lax.psum_scatter(value_sum.astype(jnp.bfloat16), ('dp', 'seq'), scatter_d...  78.4 us
    psum x1, blocking collectives, body(): lax.psum((query_gain_part, key_gain_part), ('dp', 'seq', 'tensor'))  64.6 us
  transfers between devices with their start and end apart: 16, of which 15 were waited for; matrix products, arithmetic and copies ran while one was open for 4% of the time, Pallas kernels for 0%

profile of v1, /device:TPU:0, one launch (start us, length us, event | category | flops | bytes accessed | tf_op | source)
XLA Modules:
  0.0 1142.0 jit_solution(10248904072086999529)
XLA Ops:
  8.1 26.2 %all_gather.53 = bf16[1024,128]{1,0:T(8,128)(2,1)S(1)} all-gather(bf16[32,128]{1,0:T(8,128)(2,1)} %param.24), channel_id=1, replica_groups=mesh['dp'=4,'seq'=8,'tensor'=4] {'dp','seq'}, dimensions={0}, use_global_device_ids=true | all-gather | bytes 270336 | tf_op jit(solution)/shard_map/all_gather | solution.py:80
  34.3 13.7 %all_gather.50 = bf16[256,1,1024]{2,0,1:T(8,128)(2,1)S(1)} all-gather(bf16[256,1,256]{2,0,1:T(8,128)(2,1)} %param.17), channel_id=1, replica_groups=mesh['dp'=4,'seq'=8,'tensor'=4] {'tensor'}, dimensions={2}, use_global_device_ids=true | all-gather | bytes 655360 | tf_op jit(solution)/shard_map/all_gather | solution.py:66
  51.7 63.3 %all-reduce.10 = (bf16[1024]{0:T(1024)(128)(2,1)S(1)}, bf16[1024]{0:T(1024)(128)(2,1)S(1)}) all-reduce(bf16[1024]{0:T(1024)(128)(2,1)S(1)} %dynamic-update-slice.1, bf16[1024]{0:T(1024)(128)(2,1)S(1)} %dynamic-update-slice), channel_id=1, replica_groups=mesh['dp'=4,'seq'=8,'tensor'=4] {'dp','seq'}, use_global_device_ids=true, to_apply=%add.5 | all-reduce | flops 2048 | bytes 8192
  116.5 22.4 %all_gather.52 = bf16[1024,128]{1,0:T(8,128)(2,1)S(1)} all-gather(bf16[32,128]{1,0:T(8,128)(2,1)} %param.23), channel_id=1, replica_groups=mesh['dp'=4,'seq'=8,'tensor'=4] {'dp','seq'}, dimensions={0}, use_global_device_ids=true | all-gather | bytes 270336 | tf_op jit(solution)/shard_map/all_gather | solution.py:79
  141.7 24.2 %all_gather.55 = bf16[1024,256]{1,0:T(8,128)(2,1)S(1)} all-gather(bf16[32,256]{1,0:T(8,128)(2,1)S(1)} %copy-done.38), channel_id=1, replica_groups=mesh['dp'=4,'seq'=8,'tensor'=4] {'dp','seq'}, dimensions={0}, use_global_device_ids=true | all-gather | bytes 540672 | tf_op jit(solution)/shard_map/all_gather | solution.py:78
  167.4 22.6 %all_gather.56 = bf16[1024,256]{1,0:T(8,128)(2,1)S(1)} all-gather(bf16[32,256]{1,0:T(8,128)(2,1)S(1)} %copy-done.39), channel_id=1, replica_groups=mesh['dp'=4,'seq'=8,'tensor'=4] {'dp','seq'}, dimensions={0}, use_global_device_ids=true | all-gather | bytes 540672 | tf_op jit(solution)/shard_map/all_gather | solution.py:81
  190.0 8.4 conditional.2
  192.4 2.4 fusion
  194.8 1.8 fusion.4
  196.6 1.8 fusion.9
  202.2 14.0 %all_gather.61 = bf16[256,1,1024]{2,0,1:T(8,128)(2,1)S(1)} all-gather(bf16[256,1,256]{2,0,1:T(8,128)(2,1)S(1)} %copy-done.31), channel_id=1, replica_groups=mesh['dp'=4,'seq'=8,'tensor'=4] {'tensor'}, dimensions={2}, use_global_device_ids=true | all-gather | bytes 655360 | tf_op jit(solution)/shard_map/all_gather | solution.py:198
  216.2 26.8 %all-reduce.14.cloned.1.call-done = bf16[256,1024]{1,0:T(8,128)(2,1)} async-done(((bf16[256,1024]{1,0:T(8,128)(2,1)}), bf16[256,1024]{1,0:T(8,128)(2,1)}) %all-reduce.14.cloned.1.call-update) | async-done | bytes 524304 | tf_op jit(solution)/shard_map/psum | solution.py:170
  246.1 3.6 fusion.105
  249.7 42.1 %all-gather.11.cloned.1.call-done = bf16[1024,1152]{1,0:T(8,128)(2,1)} async-done(((bf16[32,1152]{1,0:T(8,128)(2,1)}), bf16[1024,1152]{1,0:T(8,128)(2,1)}) %all-gather.11.cloned.1.call-update) | async-done | bytes 2359312 | tf_op jit(solution)/shard_map/all_gather | solution.py:83
  291.9 3.6 fusion.106
  295.4 42.2 %all-gather.13.cloned.1.call-done = bf16[1024,1152]{1,0:T(8,128)(2,1)} async-done(((bf16[32,1152]{1,0:T(8,128)(2,1)}), bf16[1024,1152]{1,0:T(8,128)(2,1)}) %all-gather.13.cloned.1.call-update) | async-done | bytes 2359312 | tf_op jit(solution)/shard_map/all_gather | solution.py:84
  337.6 4.4 multiply_convert_fusion
  344.1 1.7 fusion.47
  346.1 42.2 %all-reduce.16.cloned.1.call-done = bf16[256,1024]{1,0:T(8,128)(2,1)} async-done(((bf16[256,1024]{1,0:T(8,128)(2,1)}), bf16[256,1024]{1,0:T(8,128)(2,1)}) %all-reduce.16.cloned.1.call-update) | async-done | bytes 524304 | tf_op jit(solution)/shard_map/psum | solution.py:205
  388.2 2.1 fusion.57
  391.0 2.4 fusion.69
  393.8 14.6 %conditional.3 = (bf16[2048,1,256]{0,2,1:T(8,128)(2,1)}, f32[256,1,4,32]{0,3,2,1:T(8,128)S(1)}, f32[256,1,4,32]{0,3,2,1:T(8,128)S(1)}, f32[256,1,4,32]{0,3,2,1:T(8,128)S(1)}) conditional(s32[]{:T(128)} %convert_element_type.245, () %tuple.37, (s32[256]{0:T(256)}, bf16[2048,1,256]{0,2,1:T(8,128)(2,1)}, bf16[256,1,2,2,64]{0,4,3,2,1:T(8,128)(2,1)}, ...), branch_computations={%region_12.13_spmd, %region_13.15_spmd} | conditional | flops 1366589440 | bytes 52212880 | solution.py:261
  395.9 2.2 fusion.40
  399.2 1.9 fusion.27
  401.2 2.9 fusion.18
  404.1 2.3 fusion.33
  409.0 3.6 fusion.50
  417.8 23.5 %reduce-scatter.14.cloned.1.call-done = bf16[256,1,256]{0,2,1:T(8,128)(2,1)} async-done(((bf16[2048,1,256]{0,2,1:T(8,128)(2,1)}), bf16[256,1,256]{0,2,1:T(8,128)(2,1)}) %reduce-scatter.14.cloned.1.call-update) | async-done | bytes 131088 | tf_op jit(solution)/shard_map/reduce_scatter | solution.py:264
  445.0 3.3 fusion.44
  448.3 4.3 copy.50
  453.7 2.3 convolution_convert_fusion.2
  456.4 2.3 convolution_convert_fusion.1
  462.0 1.7 reduce-scatter.12.cloned.1.call-done
  463.6 1.7 fusion.77
  465.3 78.5 %reduce-scatter.16.cloned.1.call-done = bf16[32,256]{1,0:T(8,128)(2,1)} async-done(((bf16[1024,256]{1,0:T(8,128)(2,1)}), bf16[32,256]{1,0:T(8,128)(2,1)}) %reduce-scatter.16.cloned.1.call-update) | async-done | bytes 16400 | tf_op jit(solution)/shard_map/reduce_scatter | solution.py:300
  545.2 78.5 %reduce-scatter.22.cloned.1.call-done = bf16[32,256]{1,0:T(8,128)(2,1)} async-done(((bf16[1024,256]{1,0:T(8,128)(2,1)}), bf16[32,256]{1,0:T(8,128)(2,1)}) %reduce-scatter.22.cloned.1.call-update) | async-done | bytes 16400 | tf_op jit(solution)/shard_map/reduce_scatter | solution.py:309
  625.0 64.6 %all-reduce.8 = (f32[64]{0:T(128)}, f32[64]{0:T(128)}) all-reduce(f32[64]{0:T(128)S(1)} %copy-done.54, f32[64]{0:T(128)S(1)} %get-tuple-element.149), channel_id=1, replica_groups=mesh['dp'=4,'seq'=8,'tensor'=4] {'dp','seq','tensor'}, use_global_device_ids=true, to_apply=%region_25.26 | all-reduce | flops 128 | bytes 1024 | tf_op jit(solution)/shard_map/psum | solution.py:322
  689.6 13.8 %reduce-scatter.18.cloned.1.call-done = bf16[32,128]{1,0:T(8,128)(2,1)} async-done(((bf16[1024,128]{1,0:T(8,128)(2,1)}), bf16[32,128]{1,0:T(8,128)(2,1)}) %reduce-scatter.18.cloned.1.call-update) | async-done | bytes 8208 | tf_op jit(solution)/shard_map/reduce_scatter | solution.py:303
  704.6 78.4 %reduce-scatter.20.cloned.1.call-done = bf16[32,128]{1,0:T(8,128)(2,1)} async-done(((bf16[1024,128]{1,0:T(8,128)(2,1)}), bf16[32,128]{1,0:T(8,128)(2,1)}) %reduce-scatter.20.cloned.1.call-update) | async-done | bytes 8208 | tf_op jit(solution)/shard_map/reduce_scatter | solution.py:306
  784.3 80.8 %reduce-scatter.28.cloned.1.call-done = bf16[32,1152]{1,0:T(8,128)(2,1)} async-done(((bf16[1024,1152]{1,0:T(8,128)(2,1)}), bf16[32,1152]{1,0:T(8,128)(2,1)}) %reduce-scatter.28.cloned.1.call-update) | async-done | bytes 73744
  867.0 80.7 %reduce-scatter.24.cloned.1.call-done = bf16[32,1152]{1,0:T(8,128)(2,1)} async-done(((bf16[1024,1152]{1,0:T(8,128)(2,1)}), bf16[32,1152]{1,0:T(8,128)(2,1)}) %reduce-scatter.24.cloned.1.call-update) | async-done | bytes 73744 | tf_op jit(solution)/shard_map/reduce_scatter | solution.py:312
  947.7 1.6 convert_element_type.298
  949.3 80.5 %reduce-scatter.26.cloned.1.call-done = bf16[32,1152]{1,0:T(8,128)(2,1)} async-done(((bf16[1024,1152]{1,0:T(8,128)(2,1)}), bf16[32,1152]{1,0:T(8,128)(2,1)}) %reduce-scatter.26.cloned.1.call-update) | async-done | bytes 73744 | tf_op jit(solution)/shard_map/reduce_scatter | solution.py:315
  1029.8 1.6 convert_element_type.300
  1031.4 30.4 %all-gather.15.cloned.1.call-done = bf16[1024,1024]{1,0:T(8,128)(2,1)} async-done(((bf16[256,1024]{1,0:T(8,128)(2,1)}), bf16[1024,1024]{1,0:T(8,128)(2,1)}) %all-gather.15.cloned.1.call-update) | async-done | bytes 2097168 | tf_op jit(solution)/shard_map/all_gather | solution.py:13
  1061.7 2.0 reduce_sum.154
  1065.1 67.2 %all-reduce.9 = (bf16[1024]{0:T(1024)(128)(2,1)S(1)}, bf16[1024]{0:T(1024)(128)(2,1)S(1)}) all-reduce(bf16[1024]{0:T(1024)(128)(2,1)S(1)} %get-tuple-element.145, bf16[1024]{0:T(1024)(128)(2,1)S(1)} %copy-done.49), channel_id=5, replica_groups=mesh['dp'=4,'seq'=8,'tensor'=4] {'dp','seq'}, use_global_device_ids=true, to_apply=%region_21.22.clone | all-reduce | flops 2048 | bytes 8192
  1132.4 1.7 fusion.82
  (221 shorter events, 48.7 us)
Async XLA Ops:
  8.0 182.0 %all-gather.7.cloned.1.call-start = ((), (), s32[]{:S(2)}) async-start(), calls=%async_computation.9 | async-start | bytes 1179648 | tf_op jit(solution)/shard_map/all_gather | solution.py:147
  34.3 106.7 %copy-start.16 = (bf16[1024,128]{1,0:T(8,128)(2,1)}, bf16[1024,128]{1,0:T(8,128)(2,1)S(1)}, u32[]{:S(2)}) copy-start(bf16[1024,128]{1,0:T(8,128)(2,1)S(1)} %all_gather.53) | copy-start | bytes 786436
  34.3 106.8 %copy-start.55 = (bf16[64]{0:T(256)(128)(2,1)S(1)}, bf16[64]{0:T(256)(128)(2,1)}, u32[]{:S(2)}) copy-start(bf16[64]{0:T(256)(128)(2,1)} %param.20) | copy-start | bytes 388
  34.3 107.4 %copy-start.38 = (bf16[32,256]{1,0:T(8,128)(2,1)S(1)}, bf16[32,256]{1,0:T(8,128)(2,1)}, u32[]{:S(2)}) copy-start(bf16[32,256]{1,0:T(8,128)(2,1)} %param.22) | copy-start | bytes 49156
  115.1 50.9 %copy-start.36 = (f32[1024]{0:T(1024)}, f32[1024]{0:T(1024)S(1)}, u32[]{:S(2)}) copy-start(f32[1024]{0:T(1024)S(1)} %convert_element_type.246) | copy-start | bytes 12292
  115.8 50.6 %copy-start.43 = (f32[256]{0:T(256)}, f32[256]{0:T(256)S(1)}, u32[]{:S(2)}) copy-start(f32[256]{0:T(256)S(1)} %fusion.89) | copy-start | bytes 3076
  116.5 23.6 %copy-start.50 = (f32[64]{0:T(128)}, f32[64]{0:T(128)S(1)}, u32[]{:S(2)}) copy-start(f32[64]{0:T(128)S(1)} %convert_element_type.248) | copy-start | bytes 772
  139.7 27.7 %copy-start.39 = (bf16[32,256]{1,0:T(8,128)(2,1)S(1)}, bf16[32,256]{1,0:T(8,128)(2,1)}, u32[]{:S(2)}) copy-start(bf16[32,256]{1,0:T(8,128)(2,1)} %param.25) | copy-start | bytes 49156
  140.0 50.0 %copy-start.20 = (f32[256,32]{0,1:T(8,128)}, f32[256,32]{0,1:T(8,128)S(1)}, u32[]{:S(2)}) copy-start(f32[256,32]{0,1:T(8,128)S(1)} %get-tuple-element.184) | copy-start | bytes 98308
  140.0 50.0 %copy-start.22 = (f32[256,32]{0,1:T(8,128)}, f32[256,32]{0,1:T(8,128)S(1)}, u32[]{:S(2)}) copy-start(f32[256,32]{0,1:T(8,128)S(1)} %get-tuple-element.185) | copy-start | bytes 98308
  141.0 101.9 %all-reduce.14.cloned.1.call-start = ((), (), s32[]{:S(2)}) async-start(), calls=%async_computation.10 | async-start | bytes 1048576 | tf_op jit(solution)/shard_map/psum | solution.py:170
  141.1 48.9 %copy-start.52 = (f32[64]{0:T(128)}, f32[64]{0:T(128)S(1)}, u32[]{:S(2)}) copy-start(f32[64]{0:T(128)S(1)} %convert_element_type.252) | copy-start | bytes 772
  190.0 9.2 copy-start.3
  198.4 3.7 copy-start.40
  198.4 3.7 copy-start.31
  199.2 46.4 %copy-start.13 = (bf16[256,1,2,2,64]{0,4,3,2,1:T(8,128)(2,1)}, bf16[256,1,2,2,64]{0,4,3,2,1:T(8,128)(2,1)S(1)}, u32[]{:S(2)}) copy-start(bf16[256,1,2,2,64]{0,4,3,2,1:T(8,128)(2,1)S(1)} %get-tuple-element.159) | copy-start | bytes 393220
  200.4 45.8 %all-gather.9.cloned.1.call-start = ((), (), s32[]{:S(2)}) async-start(), calls=%async_computation.11 | async-start | bytes 2433024 | tf_op jit(solution)/shard_map/all_gather | solution.py:82
  200.9 90.9 %all-gather.11.cloned.1.call-start = ((), (), s32[]{:S(2)}) async-start(), calls=%async_computation.12 | async-start | bytes 2433024 | tf_op jit(solution)/shard_map/all_gather | solution.py:83
  201.5 136.1 %all-gather.13.cloned.1.call-start = ((), (), s32[]{:S(2)}) async-start(), calls=%async_computation.13 | async-start | bytes 2433024 | tf_op jit(solution)/shard_map/all_gather | solution.py:84
  202.1 186.1 %all-reduce.16.cloned.1.call-start = ((), (), s32[]{:S(2)}) async-start(), calls=%async_computation.15 | async-start | bytes 1048576 | tf_op jit(solution)/shard_map/psum | solution.py:205
  244.2 5.5 copy-start.48
  244.3 5.5 copy-start.42
  337.6 4.4 copy-start
  344.1 44.1 %copy-start.2 = (bf16[256,1024]{1,0:T(8,128)(2,1)S(1)}, bf16[256,1024]{1,0:T(8,128)(2,1)}, u32[]{:S(2)}) copy-start(bf16[256,1024]{1,0:T(8,128)(2,1)} %all-reduce.14.cloned.1.call-done) | copy-start | bytes 1572868
  345.8 95.5 %reduce-scatter.14.cloned.1.call-start = ((), (), s32[]{:S(2)}) async-start(), calls=%async_computation.16 | async-start | bytes 1179648 | tf_op jit(solution)/shard_map/reduce_scatter | solution.py:264
  408.3 4.2 copy-start.27
  408.4 4.2 copy-start.28
  408.4 4.3 copy-start.21
  408.4 4.2 copy-start.23
  408.4 55.2 %reduce-scatter.12.cloned.1.call-start = ((), (), s32[]{:S(2)}) async-start(), calls=%async_computation.14 | async-start | bytes 655360 | tf_op jit(solution)/shard_map/reduce_scatter | solution.py:178
  409.0 4.7 copy-start.53
  409.0 6.2 copy-start.37
  409.0 6.2 copy-start.44
  412.6 4.0 copy-start.14
  412.6 131.3 %reduce-scatter.16.cloned.1.call-start = ((), (), s32[]{:S(2)}) async-start(), calls=%async_computation.17 | async-start | bytes 540672 | tf_op jit(solution)/shard_map/reduce_scatter | solution.py:300
  414.5 27.7 %copy-start.33 = (f32[256,2]{0,1:T(2,128)S(1)}, f32[256,2]{0,1:T(2,128)}, u32[]{:S(2)}) copy-start(f32[256,2]{0,1:T(2,128)} %copy-done.32) | copy-start | bytes 6148
  414.6 27.7 %copy-start.51 = (f32[64]{0:T(128)S(1)}, f32[64]{0:T(128)}, u32[]{:S(2)}) copy-start(f32[64]{0:T(128)} %copy-done.50) | copy-start | bytes 772
  415.2 27.2 %copy-start.35 = (f32[256,2]{0,1:T(2,128)S(1)}, f32[256,2]{0,1:T(2,128)}, u32[]{:S(2)}) copy-start(f32[256,2]{0,1:T(2,128)} %copy-done.34) | copy-start | bytes 6148
  415.2 27.3 %copy-start.45 = (f32[256]{0:T(256)S(1)}, f32[256]{0:T(256)}, u32[]{:S(2)}) copy-start(f32[256]{0:T(256)} %copy-done.43) | copy-start | bytes 3076
  416.5 207.2 %reduce-scatter.22.cloned.1.call-start = ((), (), s32[]{:S(2)}) async-start(), calls=%async_computation.20 | async-start | bytes 540672 | tf_op jit(solution)/shard_map/reduce_scatter | solution.py:309
  417.8 285.6 %reduce-scatter.18.cloned.1.call-start = ((), (), s32[]{:S(2)}) async-start(), calls=%async_computation.18 | async-start | bytes 270336 | tf_op jit(solution)/shard_map/reduce_scatter | solution.py:303
  443.7 339.3 %reduce-scatter.20.cloned.1.call-start = ((), (), s32[]{:S(2)}) async-start(), calls=%async_computation.19 | async-start | bytes 270336 | tf_op jit(solution)/shard_map/reduce_scatter | solution.py:306
  444.9 420.2 %reduce-scatter.28.cloned.1.call-start = ((), (), s32[]{:S(2)}) async-start(), calls=%async_computation.24 | async-start | bytes 2433024
  452.6 3.7 copy-start.6
  452.6 495.1 %reduce-scatter.24.cloned.1.call-start = ((), (), s32[]{:S(2)}) async-start(), calls=%async_computation.21 | async-start | bytes 2433024 | tf_op jit(solution)/shard_map/reduce_scatter | solution.py:312
  456.0 573.8 %reduce-scatter.26.cloned.1.call-start = ((), (), s32[]{:S(2)}) async-start(), calls=%async_computation.22 | async-start | bytes 2433024 | tf_op jit(solution)/shard_map/reduce_scatter | solution.py:315
  458.7 603.0 %all-gather.15.cloned.1.call-start = ((), (), s32[]{:S(2)}) async-start(), calls=%async_computation.23 | async-start | bytes 2621440 | tf_op jit(solution)/shard_map/all_gather | solution.py:13
  460.0 165.0 %copy-start.54 = (f32[64]{0:T(128)S(1)}, f32[64]{0:T(128)}, u32[]{:S(2)}) copy-start(f32[64]{0:T(128)} %get-tuple-element.147) | copy-start | bytes 772
  (24 other events, 37.6 us)
Sparse Core Ops, SparseCore 0:
  141.2 22.5 all-gather.6
  200.5 42.4 all-reduce.13
  345.9 42.2 all-reduce.15
  408.5 32.7 reduce-scatter.13
  443.5 20.0 reduce-scatter.11
  466.9 76.8 reduce-scatter.15
  547.3 76.3 reduce-scatter.21
  627.1 76.2 reduce-scatter.17
  706.8 76.2 reduce-scatter.19
  786.4 78.6 reduce-scatter.27
  869.1 78.5 reduce-scatter.23
  951.2 78.5 reduce-scatter.25
  1031.6 30.1 all-gather.14
Sparse Core Ops, SparseCore 1:
  203.1 43.0 all-gather.8
  248.2 43.6 all-gather.10
  294.0 43.6 all-gather.12
